TPU v7x, 32 devices: a whole 2x2x4 slice. The times are simulated.
32 devices in a mesh: groups: 2 (over y), space: 4 (over z), tm: 2 (over x), chan: 2 (over core).
Axes of the slice: x: 2, y: 2, z: 4, core: 2. Of those that a mesh axis runs over, the one named last changes fastest.
Arguments:
- hidden_states: bfloat16 [8, 4, 64, 512], P(('groups', 'tm'), 'space', None, 'chan'), parts along dimension 0, may hold values from -25 to 25
- first_gain: float32 [512], P('chan'), may hold values from 0.1 to 1.9
- second_gain: float32 [512], P('chan'), may hold values from 0.1 to 1.9
- query_weight: bfloat16 [512, 512], replicated, may hold values from -0.4861359 to 0.4861359
- key_weight: bfloat16 [512, 512], replicated, may hold values from -0.4861359 to 0.4861359
- value_weight: bfloat16 [512, 512], replicated, may hold values from -0.25 to 0.25
- out_weight: bfloat16 [512, 512], replicated, may hold values from -0.25 to 0.25
- conv_kernel: bfloat16 [3, 3, 3, 512, 512], P(None, None, None, 'tm', 'chan'), may hold values from -0.0546875 to 0.0546875
Outputs:
- attended: bfloat16 [8, 4, 64, 512], P(('groups', 'tm'), 'space', None, 'chan'), parts along dimension 0
- convolved: bfloat16 [8, 4, 64, 512], P(('groups', 'tm'), 'space', None, 'chan'), parts along dimension 0
There are 2 independent parts, one for each index of `groups`. A program takes and returns all parts, laid end to end along the dimension named above; an argument that names none is the same for every part. Nothing has to cross between parts.
All inputs are finite; a program needn't handle non-finite values.
Results may differ from a plain program's by a relative error of at most 0.012.
The roundings to bfloat16 on the way count: a program that leaves them out, or rounds other values in their place, can miss the bound.
Values may be sent and summed in bfloat16 or wider, within the bound.
A program may use at most 64 MiB of HBM per device.

v0:
```python
import jax
import jax.numpy as jnp
from jax import lax
from jax.sharding import PartitionSpec as P

D = 512
NGROUP = 32
EPSILON = 1e-06


def shifted_2(x, axis, by):
    peers = lax.axis_size(axis)
    pairs = [(i, i + by) for i in range(peers) if 0 <= i + by < peers]
    return lax.ppermute(x, axis, pairs)


def padded_2(cells, sides, width):
    for axis, dim in sides:
        count = lax.axis_size(axis)
        ends = count - 1
        head = lax.slice_in_dim(cells, 0, width, axis=dim)
        tail = lax.slice_in_dim(cells, cells.shape[dim] - width, cells.shape[dim], axis=dim)
        cells = jnp.concatenate(
            [
                lax.ppermute(tail, axis, [(i, (i + 1) % count) for i in range(ends)]),
                cells,
                lax.ppermute(head, axis, [((i + 1) % count, i) for i in range(ends)]),
            ],
            axis=dim,
        )
    return cells


def normalize(source, gain_vector):
    channels = source.shape[3]
    group_width = D // NGROUP
    grouped = source.reshape(-1, channels // group_width, group_width)
    population = grouped.shape[0] * group_width * lax.axis_size("space") * lax.axis_size("tm")
    group_sums, group_squares = lax.psum(
        (jnp.sum(grouped, axis=(0, 2)), jnp.sum(grouped * grouped, axis=(0, 2))), ("space", "tm")
    )
    centre = group_sums / population
    spread = jnp.maximum(group_squares / population - centre * centre, 0.0)
    shifted = grouped - centre[None, :, None]
    scaled = shifted * lax.rsqrt(spread + EPSILON)[None, :, None]
    return scaled.reshape(source.shape) * gain_vector


def attend(normed, query_weight, key_weight, value_weight, out_weight):
    frame_count, row_count, col_count, channels = normed.shape
    token_count = frame_count * row_count * col_count
    tokens = normed.reshape(token_count, channels)
    halves = lax.all_to_all(tokens, "chan", split_axis=0, concat_axis=1, tiled=True)
    half_rows = halves.shape[0]
    queries = jnp.dot(halves, query_weight, preferred_element_type=jnp.float32).astype(jnp.bfloat16)
    keyed = jnp.dot(halves, key_weight, preferred_element_type=jnp.float32).astype(jnp.bfloat16)
    valued = jnp.dot(halves, value_weight, preferred_element_type=jnp.float32).astype(jnp.bfloat16)
    score_scale = D ** (-0.5)
    running_max = jnp.full((half_rows,), -1e30, jnp.float32)
    key_piece = lax.all_gather(keyed, "space", axis=0, tiled=True)
    value_piece = lax.all_gather(valued, "space", axis=0, tiled=True)
    scores = jnp.dot(queries, key_piece.T, preferred_element_type=jnp.float32) * score_scale
    newest_max = jnp.maximum(running_max, jnp.max(scores, axis=1))
    weights = jnp.exp(scores - newest_max[:, None])
    running_sum = jnp.sum(weights, axis=1)
    accumulated = jnp.dot(
        weights.astype(jnp.bfloat16), value_piece, preferred_element_type=jnp.float32
    )
    mixed = (accumulated / running_sum[:, None]).astype(jnp.bfloat16)
    projected = jnp.dot(mixed, out_weight, preferred_element_type=jnp.float32).astype(jnp.bfloat16)
    returned = lax.all_to_all(projected, "chan", split_axis=1, concat_axis=0, tiled=True)
    return returned.reshape(frame_count, row_count, col_count, channels)


def join_channels(activated):
    return lax.all_gather(activated, "chan", axis=3, tiled=True)


def extend(frames_in):
    earlier = shifted_2(frames_in, "tm", 1)
    timed = jnp.concatenate([earlier, frames_in], axis=0)
    rimmed = padded_2(timed, (("space", 1),), 1)
    return jnp.pad(rimmed, ((0, 0), (0, 0), (1, 1), (0, 0)))


def convolve(activated, conv_kernel):
    frame_count, row_count, col_count = (activated.shape[0], activated.shape[1], activated.shape[2])
    padded = extend(join_channels(activated))
    out_width = conv_kernel.shape[4]
    initial = jnp.zeros((frame_count * row_count * col_count, out_width), jnp.float32)
    running_total = initial
    piece = lax.all_gather(conv_kernel, "tm", axis=3, tiled=True)
    for time_tap in range(3):
        for row_tap in range(3):
            for col_tap in range(3):
                window = padded[
                    time_tap : time_tap + frame_count,
                    row_tap : row_tap + row_count,
                    col_tap : col_tap + col_count,
                ]
                window = window.reshape(frame_count * row_count * col_count, piece.shape[3])
                running_total = running_total + jnp.dot(
                    window, piece[time_tap, row_tap, col_tap], preferred_element_type=jnp.float32
                )
    return running_total.reshape(frame_count, row_count, col_count, out_width).astype(jnp.bfloat16)


def on_device(
    hidden_states,
    first_gain,
    second_gain,
    query_weight,
    key_weight,
    value_weight,
    out_weight,
    conv_kernel,
):
    source = hidden_states.astype(jnp.float32)
    normed = normalize(source, first_gain).astype(jnp.bfloat16)
    attended = attend(normed, query_weight, key_weight, value_weight, out_weight)
    resid = source + attended.astype(jnp.float32)
    activated = jax.nn.silu(normalize(resid, second_gain)).astype(jnp.bfloat16)
    convolved = convolve(activated, conv_kernel)
    return (attended, convolved)


def solution(mesh):
    placed = (
        P(("groups", "tm"), "space", None, "chan"),
        P("chan"),
        P("chan"),
        P(),
        P(),
        P(),
        P(),
        P(None, None, None, "tm", "chan"),
    )
    return jax.shard_map(
        on_device,
        mesh=mesh,
        in_specs=placed,
        out_specs=(
            P(("groups", "tm"), "space", None, "chan"),
            P(("groups", "tm"), "space", None, "chan"),
        ),
        check_vma=False,
    )
```

profile of v0, /device:TPU:0, one launch (start us, length us, event | category | flops | bytes accessed | tf_op | source)
XLA Modules:
  0.0 143.7 jit_solution(14035605134556565551)
XLA Ops:
  9.2 23.3 %all-reduce.2 = (f32[16]{0:T(128)S(1)}, f32[16]{0:T(128)S(1)}) all-reduce(f32[16]{0:T(128)S(1)} %reduce_sum.62, f32[16]{0:T(128)S(1)} %reduce_sum.59), channel_id=1, replica_groups=mesh['groups'=2,'space'=4,'tm'=2,'chan'=2] {'space','tm'}, use_global_device_ids=true, to_apply=%region_5.0 | all-reduce | flops 32 | bytes 256 | tf_op jit(solution)/shard_map/psum | solution.py:39
  33.7 3.8 %all_to_all.35 = bf16[2,64,256]{2,1,0:T(8,128)(2,1)S(1)} all-to-all(bf16[2,64,256]{2,1,0:T(8,128)(2,1)S(1)} %fusion.26), channel_id=1, replica_groups=mesh['groups'=2,'space'=4,'tm'=2,'chan'=2] {'chan'}, dimensions={0} | all-to-all | bytes 131072 | tf_op jit(solution)/shard_map/all_to_all | solution.py:53
  37.8 14.3 %all_gather.12 = bf16[256,512]{1,0:T(8,128)(2,1)S(1)} all-gather(bf16[64,512]{1,0:T(8,128)(2,1)S(1)} %convolution_convert_fusion.2), channel_id=1, replica_groups=mesh['groups'=2,'space'=4,'tm'=2,'chan'=2] {'space'}, dimensions={0}, use_global_device_ids=true | all-gather | bytes 327680 | tf_op jit(solution)/shard_map/all_gather | solution.py:60
  52.1 1.2 convolution_convert_fusion.1
  53.3 13.9 %all_gather.13 = bf16[256,512]{1,0:T(8,128)(2,1)S(1)} all-gather(bf16[64,512]{1,0:T(8,128)(2,1)S(1)} %convolution_convert_fusion.1), channel_id=1, replica_groups=mesh['groups'=2,'space'=4,'tm'=2,'chan'=2] {'space'}, dimensions={0}, use_global_device_ids=true | all-gather | bytes 327680 | tf_op jit(solution)/shard_map/all_gather | solution.py:61
  67.2 1.5 %fusion.37 = (f32[64]{0:T(128)S(1)}, f32[64,256]{1,0:T(8,128)S(1)}) fusion(bf16[256,512]{1,0:T(8,128)(2,1)S(1)} %all_gather.12, bf16[64,512]{1,0:T(8,128)(2,1)S(1)} %bitcast.164, bf16[512,512]{1,0:T(8,128)(2,1)} %param.11), kind=kOutput, calls=%fused_computation.104 | convolution fusion | flops 50397120 | bytes 917760 | tf_op jit(solution)/shard_map/dot_general | solution.py:62
  68.9 1.4 convolution_convert_fusion
  70.3 3.8 %all_to_all.36 = bf16[64,2,256]{2,0,1:T(8,128)(2,1)S(1)} all-to-all(bf16[64,2,256]{2,0,1:T(8,128)(2,1)S(1)} %bitcast.193), channel_id=1, replica_groups=mesh['groups'=2,'space'=4,'tm'=2,'chan'=2] {'chan'}, dimensions={1} | all-to-all | bytes 131072 | tf_op jit(solution)/shard_map/all_to_all | solution.py:71
  74.6 17.4 %all-reduce.1 = (f32[16]{0:T(128)S(1)}, f32[16]{0:T(128)S(1)}) all-reduce(f32[16]{0:T(128)S(1)} %reduce_sum.85, f32[16]{0:T(128)S(1)} %reduce_sum.82), channel_id=1, replica_groups=mesh['groups'=2,'space'=4,'tm'=2,'chan'=2] {'space','tm'}, use_global_device_ids=true, to_apply=%region_13.14 | all-reduce | flops 32 | bytes 256 | tf_op jit(solution)/shard_map/psum | solution.py:39
  92.4 1.9 %all_gather.14 = bf16[2,1,64,512]{3,2,1,0:T(8,128)(2,1)S(1)} all-gather(bf16[2,1,64,256]{3,2,1,0:T(8,128)(2,1)S(1)} %multiply_convert_fusion), channel_id=1, replica_groups=mesh['groups'=2,'space'=4,'tm'=2,'chan'=2] {'chan'}, dimensions={3}, use_global_device_ids=true | all-gather | bytes 196608 | tf_op jit(solution)/shard_map/all_gather | solution.py:76
  94.3 4.1 %collective-permute-start = (bf16[2,1,64,512]{3,2,1,0:T(8,128)(2,1)S(1)}, bf16[2,1,64,512]{3,2,1,0:T(8,128)(2,1)S(1)}, u32[]{:S(2)}, u32[]{:S(2)}) collective-permute-start(bf16[2,1,64,512]{3,2,1,0:T(8,128)(2,1)S(1)} %all_gather.14), channel_id=1, source_target_pairs={{0,2},{1,3},{4,6},{5,7},{8,10},{9,11},{12,14},{13,15},{16,18},{17,... | collective-permute-start | bytes 393224 | tf_op jit(solution)/shard_map/ppermute | solution.py:14
  98.4 4.3 %collective-permute-done = bf16[2,1,64,512]{3,2,1,0:T(8,128)(2,1)S(1)} collective-permute-done((bf16[2,1,64,512]{3,2,1,0:T(8,128)(2,1)S(1)}, bf16[2,1,64,512]{3,2,1,0:T(8,128)(2,1)S(1)}, u32[]{:S(2)}, u32[]{:S(2)}) %collective-permute-start) | collective-permute-done | bytes 131104 | tf_op jit(solution)/shard_map/ppermute | solution.py:14
  102.8 3.0 %collective-permute-start.1 = (bf16[4,1,64,512]{3,2,1,0:T(8,128)(2,1)S(1)}, bf16[4,1,64,512]{3,2,1,0:T(8,128)(2,1)S(1)}, u32[]{:S(2)}, u32[]{:S(2)}) collective-permute-start(bf16[4,1,64,512]{3,2,1,0:T(8,128)(2,1)S(1)} %constant_dynamic-update-slice_fusion), channel_id=1, source_target_pairs={{0,4},{4,8},{8,12},{1,5},{5,9},{9,13},{2,6},{6,10},{10,14},{3,7},{... | collective-permute-start | bytes 786440 | tf_op jit(solution)/shard_map/ppermute | solution.py:25
  105.8 1.3 collective-permute-start.2
  107.1 3.8 %collective-permute-done.1 = bf16[4,1,64,512]{3,2,1,0:T(8,128)(2,1)S(1)} collective-permute-done((bf16[4,1,64,512]{3,2,1,0:T(8,128)(2,1)S(1)}, bf16[4,1,64,512]{3,2,1,0:T(8,128)(2,1)S(1)}, u32[]{:S(2)}, u32[]{:S(2)}) %collective-permute-start.1) | collective-permute-done | bytes 262176 | tf_op jit(solution)/shard_map/ppermute | solution.py:25
  110.9 4.1 %collective-permute-done.2 = bf16[4,1,64,512]{3,2,1,0:T(8,128)(2,1)S(1)} collective-permute-done((bf16[4,1,64,512]{3,2,1,0:T(8,128)(2,1)S(1)}, bf16[4,1,64,512]{3,2,1,0:T(8,128)(2,1)S(1)}, u32[]{:S(2)}, u32[]{:S(2)}) %collective-permute-start.2) | collective-permute-done | bytes 262176 | tf_op jit(solution)/shard_map/ppermute | solution.py:27
  117.2 1.3 fusion.20
  118.5 1.7 %fusion.19 = f32[128,256]{1,0:T(8,128)S(1)} fusion(bf16[128,512]{1,0:T(8,128)(2,1)S(1)} %bitcast.184, bf16[3,3,3,512,256]{4,3,2,1,0:T(8,128)(2,1)} %all-gather.2.cloned.1.call-done), kind=kOutput, calls=%fused_computation.69 | convolution fusion | flops 33554432 | bytes 524288 | tf_op jit(solution)/shard_map/dot_general | solution.py:102
  120.2 1.1 fusion.18
  123.7 1.2 fusion.15
  124.8 1.1 fusion.14
  126.0 1.1 convolution_add_fusion.19
  127.1 1.1 convolution_add_fusion.18
  130.6 1.1 convolution_add_fusion.15
  (73 shorter events, 16.2 us)
Async XLA Ops:
  7.2 30.4 %copy-start = (bf16[512,512]{1,0:T(8,128)(2,1)S(1)}, bf16[512,512]{1,0:T(8,128)(2,1)}, u32[]{:S(2)}) copy-start(bf16[512,512]{1,0:T(8,128)(2,1)} %param.12) | copy-start | bytes 1572868
  7.2 67.0 %copy-start.2 = (bf16[2,1,64,256]{3,2,1,0:T(8,128)(2,1)S(1)}, bf16[2,1,64,256]{3,2,1,0:T(8,128)(2,1)}, u32[]{:S(2)}) copy-start(bf16[2,1,64,256]{3,2,1,0:T(8,128)(2,1)} %param.8) | copy-start | bytes 196612
  7.2 85.1 %copy-start.7 = (f32[256]{0:T(256)S(1)}, f32[256]{0:T(256)}, u32[]{:S(2)}) copy-start(f32[256]{0:T(256)} %param.10) | copy-start | bytes 3076
  7.2 110.0 %all-gather.2.cloned.1.call-start = ((), (), s32[]{:S(2)}) async-start(), calls=%async_computation.2 | async-start | bytes 10616832 | tf_op jit(solution)/shard_map/all_gather | solution.py:92
  94.3 8.4 %collective-permute-start = (bf16[2,1,64,512]{3,2,1,0:T(8,128)(2,1)S(1)}, bf16[2,1,64,512]{3,2,1,0:T(8,128)(2,1)S(1)}, u32[]{:S(2)}, u32[]{:S(2)}) collective-permute-start(bf16[2,1,64,512]{3,2,1,0:T(8,128)(2,1)S(1)} %all_gather.14), channel_id=1, source_target_pairs={{0,2},{1,3},{4,6},{5,7},{8,10},{9,11},{12,14},{13,15},{16,18},{17,... | collective-permute-start | bytes 393224 | tf_op jit(solution)/shard_map/ppermute | solution.py:14
  102.8 8.1 %collective-permute-start.1 = (bf16[4,1,64,512]{3,2,1,0:T(8,128)(2,1)S(1)}, bf16[4,1,64,512]{3,2,1,0:T(8,128)(2,1)S(1)}, u32[]{:S(2)}, u32[]{:S(2)}) collective-permute-start(bf16[4,1,64,512]{3,2,1,0:T(8,128)(2,1)S(1)} %constant_dynamic-update-slice_fusion), channel_id=1, source_target_pairs={{0,4},{4,8},{8,12},{1,5},{5,9},{9,13},{2,6},{6,10},{10,14},{3,7},{... | collective-permute-start | bytes 786440 | tf_op jit(solution)/shard_map/ppermute | solution.py:25
  105.8 9.2 %collective-permute-start.2 = (bf16[4,1,64,512]{3,2,1,0:T(8,128)(2,1)S(1)}, bf16[4,1,64,512]{3,2,1,0:T(8,128)(2,1)S(1)}, u32[]{:S(2)}, u32[]{:S(2)}) collective-permute-start(bf16[4,1,64,512]{3,2,1,0:T(8,128)(2,1)S(1)} %constant_dynamic-update-slice_fusion), channel_id=1, source_target_pairs={{4,0},{8,4},{12,8},{5,1},{9,5},{13,9},{6,2},{10,6},{14,10},{7,3},{... | collective-permute-start | bytes 786440 | tf_op jit(solution)/shard_map/ppermute | solution.py:27
  117.2 14.5 %copy-start.1 = (bf16[3,3,3,512,256]{4,3,2,1,0:T(8,128)(2,1)S(1)}, bf16[3,3,3,512,256]{4,3,2,1,0:T(8,128)(2,1)}, u32[]{:S(2)}) copy-start(bf16[3,3,3,512,256]{4,3,2,1,0:T(8,128)(2,1)} %all-gather.2.cloned.1.call-done) | copy-start | bytes 21233668
  117.2 15.8 %copy-start.6 = (bf16[2,1,64,512]{3,2,1,0:T(8,128)(2,1)S(1)}, bf16[2,1,64,512]{3,2,1,0:T(8,128)(2,1)}, u32[]{:S(2)}) copy-start(bf16[2,1,64,512]{3,2,1,0:T(8,128)(2,1)} %get-tuple-element.38) | copy-start | bytes 393220
  117.2 16.8 %copy-start.5 = (bf16[2,1,64,512]{3,2,1,0:T(8,128)(2,1)S(1)}, bf16[2,1,64,512]{3,2,1,0:T(8,128)(2,1)}, u32[]{:S(2)}) copy-start(bf16[2,1,64,512]{3,2,1,0:T(8,128)(2,1)} %get-tuple-element.35) | copy-start | bytes 393220
  117.2 17.2 %copy-start.4 = (bf16[2,1,64,512]{3,2,1,0:T(8,128)(2,1)S(1)}, bf16[2,1,64,512]{3,2,1,0:T(8,128)(2,1)}, u32[]{:S(2)}) copy-start(bf16[2,1,64,512]{3,2,1,0:T(8,128)(2,1)} %get-tuple-element.37) | copy-start | bytes 393220
  123.6 11.8 %copy-start.3 = (bf16[2,1,64,512]{3,2,1,0:T(8,128)(2,1)S(1)}, bf16[2,1,64,512]{3,2,1,0:T(8,128)(2,1)}, u32[]{:S(2)}) copy-start(bf16[2,1,64,512]{3,2,1,0:T(8,128)(2,1)} %get-tuple-element.34) | copy-start | bytes 393220
Sparse Core Ops, SparseCore 0:
  9.6 92.6 all-gather.1
where the time goes:
time: 145 us; the launch traced here: 144 us
  blocking collectives  78.5 us (54%)
  matrix products  23.1 us (16%)
  between operations  14.5 us (10%)
  waiting for transfers between devices  12.9 us (9%)
  starting transfers between devices  8.43 us (6%)
  local copies, waits for them, and re-layouts  3.52 us (2%)
  other arithmetic  2.8 us (2%)
    psum x2, blocking collectives, normalize(): lax.psum((jnp.sum(grouped, axis=(0, 2)), jnp.sum(grouped * grouped, axis=...  40.8 us
    dot_general x27, matrix products, convolve(): jnp.dot(window, piece[time_tap, row_tap, col_tap], preferred_element_type...  18.8 us
    all_gather x1, blocking collectives, attend(): key_piece = lax.all_gather(keyed, 'space', axis=0, tiled=True)  14.3 us
    all_gather x1, blocking collectives, attend(): value_piece = lax.all_gather(valued, 'space', axis=0, tiled=True)  13.9 us
    ppermute x1, waiting for transfers between devices, shifted_2(): return lax.ppermute(x, axis, pairs)  4.29 us
    ppermute x1, waiting for transfers between devices, padded_2(): lax.ppermute(head, axis, [((i + 1) % count, i) for i in range(ends)])  4.13 us
    ppermute x1, starting transfers between devices, shifted_2(): return lax.ppermute(x, axis, pairs)  4.12 us
    ppermute x1, waiting for transfers between devices, padded_2(): lax.ppermute(tail, axis, [(i, (i + 1) % count) for i in range(ends)])  3.8 us
  transfers between devices with their start and end apart: 4, of which 3 were waited for; matrix products, arithmetic and copies ran while one was open for 7% of the time, Pallas kernels for 0%

commit v1 on v0

--- a/solution.py
+++ b/solution.py
@@ -6,6 +6,16 @@
 D = 512
 NGROUP = 32
 EPSILON = 1e-06
+
+
+def pass_along(x, axis, along):
+    count = lax.axis_size(axis)
+    current, parts = (x, [x])
+    for _ in range(count - 1):
+        current = lax.ppermute(current, axis, [(i, (i + 1) % count) for i in range(count)])
+        parts.insert(0, current)
+    line = jnp.concatenate(parts, axis=along)
+    return jnp.roll(line, (lax.axis_index(axis) + 1) * x.shape[along], axis=along)
 
 
 def shifted_2(x, axis, by):
@@ -58,7 +68,7 @@
     score_scale = D ** (-0.5)
     running_max = jnp.full((half_rows,), -1e30, jnp.float32)
     key_piece = lax.all_gather(keyed, "space", axis=0, tiled=True)
-    value_piece = lax.all_gather(valued, "space", axis=0, tiled=True)
+    value_piece = pass_along(valued, "space", 0)
     scores = jnp.dot(queries, key_piece.T, preferred_element_type=jnp.float32) * score_scale
     newest_max = jnp.maximum(running_max, jnp.max(scores, axis=1))
     weights = jnp.exp(scores - newest_max[:, None])

time: 145 us -> 143 us (0.986)
  blocking collectives: 78.5 us -> 64.5 us
  waiting for transfers between devices: 12.9 us -> 24.8 us
    all_gather x1 -> x0, blocking collectives: 13.9 us -> none  [attend(): value_piece = lax.all_gather(valued, 'space', axis=0, tiled=True)]
    ppermute x0 -> x3, waiting for transfers between devices: none -> 9.48 us  [pass_along(): lax.ppermute(current, axis, [(i, (i + 1) % count) for i in range(count)])]
    ppermute x0 -> x3, starting transfers between devices: none -> 2.95 us  [pass_along(): lax.ppermute(current, axis, [(i, (i + 1) % count) for i in range(count)])]
    ppermute x1, waiting for transfers between devices: 4.29 us -> 6.44 us  [shifted_2(): return lax.ppermute(x, axis, pairs)]
    ppermute x1, starting transfers between devices: 2.98 us -> 1.31 us  [padded_2(): lax.ppermute(tail, axis, [(i, (i + 1) % count) for i in range(ends)])]
  transfers between devices with their start and end apart: 4 -> 7, of which waited for: 3 -> 5; matrix products, arithmetic and copies ran while one was open for 7% -> 6% of each run, Pallas kernels for 0% -> 0%
where the time goes in v1:
time: 143 us; the launch traced here: 142 us
  blocking collectives  64.5 us (45%)
  waiting for transfers between devices  24.8 us (17%)
  matrix products  22.1 us (15%)
  between operations  14.6 us (10%)
  starting transfers between devices  9.71 us (7%)
  local copies, waits for them, and re-layouts  3.57 us (2%)
  other arithmetic  2.79 us (2%)
    psum x2, blocking collectives, normalize(): lax.psum((jnp.sum(grouped, axis=(0, 2)), jnp.sum(grouped * grouped, axis=...  40.8 us
    dot_general x27, matrix products, convolve(): jnp.dot(window, piece[time_tap, row_tap, col_tap], preferred_element_type...  18.8 us
    all_gather x1, blocking collectives, attend(): key_piece = lax.all_gather(keyed, 'space', axis=0, tiled=True)  14.3 us
    ppermute x3, waiting for transfers between devices, pass_along(): lax.ppermute(current, axis, [(i, (i + 1) % count) for i in range(count)])  9.48 us
    ppermute x1, waiting for transfers between devices, shifted_2(): return lax.ppermute(x, axis, pairs)  6.44 us
    ppermute x1, waiting for transfers between devices, padded_2(): lax.ppermute(head, axis, [((i + 1) % count, i) for i in range(ends)])  4.13 us
    ppermute x1, starting transfers between devices, shifted_2(): return lax.ppermute(x, axis, pairs)  4.12 us
    ppermute x1, waiting for transfers between devices, padded_2(): lax.ppermute(tail, axis, [(i, (i + 1) % count) for i in range(ends)])  4.08 us
  transfers between devices with their start and end apart: 7, of which 5 were waited for; matrix products, arithmetic and copies ran while one was open for 6% of the time, Pallas kernels for 0%

profile of v1, /device:TPU:0, one launch (start us, length us, event | category | flops | bytes accessed | tf_op | source)
XLA Modules:
  0.0 142.0 jit_solution(14323070120578416785)
XLA Ops:
  9.2 23.3 %all-reduce.2 = (f32[16]{0:T(128)S(1)}, f32[16]{0:T(128)S(1)}) all-reduce(f32[16]{0:T(128)S(1)} %reduce_sum.62, f32[16]{0:T(128)S(1)} %reduce_sum.59), channel_id=1, replica_groups=mesh['groups'=2,'space'=4,'tm'=2,'chan'=2] {'space','tm'}, use_global_device_ids=true, to_apply=%region_5.6 | all-reduce | flops 32 | bytes 256 | tf_op jit(solution)/shard_map/psum | solution.py:49
  33.7 3.8 %all_to_all.35 = bf16[2,64,256]{2,1,0:T(8,128)(2,1)S(1)} all-to-all(bf16[2,64,256]{2,1,0:T(8,128)(2,1)S(1)} %fusion.28), channel_id=1, replica_groups=mesh['groups'=2,'space'=4,'tm'=2,'chan'=2] {'chan'}, dimensions={0} | all-to-all | bytes 131072 | tf_op jit(solution)/shard_map/all_to_all | solution.py:63
  37.8 1.2 convolution_convert_fusion.2
  39.1 14.3 %all_gather.9 = bf16[256,512]{1,0:T(8,128)(2,1)S(1)} all-gather(bf16[64,512]{1,0:T(8,128)(2,1)S(1)} %convolution_convert_fusion.2), channel_id=1, replica_groups=mesh['groups'=2,'space'=4,'tm'=2,'chan'=2] {'space'}, dimensions={0}, use_global_device_ids=true | all-gather | bytes 327680 | tf_op jit(solution)/shard_map/all_gather | solution.py:70
  53.3 1.5 %fusion.41 = (f32[64]{0:T(128)S(1)}, f32[64,256]{1,0:T(8,128)S(1)}) fusion(bf16[256,512]{1,0:T(8,128)(2,1)S(1)} %all_gather.9, bf16[64,512]{1,0:T(8,128)(2,1)S(1)} %bitcast.163, bf16[512,512]{1,0:T(8,128)(2,1)} %param.11), kind=kOutput, calls=%fused_computation.114 | convolution fusion | flops 50397120 | bytes 917760 | tf_op jit(solution)/shard_map/dot_general | solution.py:72
  54.8 2.3 %collective-permute-start.1 = (bf16[64,512]{1,0:T(8,128)(2,1)S(1)}, bf16[64,512]{1,0:T(8,128)(2,1)S(1)}, u32[]{:S(2)}, u32[]{:S(2)}) collective-permute-start(bf16[64,512]{1,0:T(8,128)(2,1)S(1)} %collective-permute-done), channel_id=1, source_target_pairs={{0,4},{4,8},{8,12},{12,0},{1,5},{5,9},{9,13},{13,1},{2,6},{6,10},{... | collective-permute-start | bytes 196616 | tf_op jit(solution)/shard_map/ppermute | solution.py:15
  57.1 4.2 %collective-permute-done.1 = bf16[64,512]{1,0:T(8,128)(2,1)S(1)} collective-permute-done((bf16[64,512]{1,0:T(8,128)(2,1)S(1)}, bf16[64,512]{1,0:T(8,128)(2,1)S(1)}, u32[]{:S(2)}, u32[]{:S(2)}) %collective-permute-start.1) | collective-permute-done | bytes 65568 | tf_op jit(solution)/shard_map/ppermute | solution.py:15
  62.1 5.2 %collective-permute-done.2 = bf16[64,512]{1,0:T(8,128)(2,1)S(1)} collective-permute-done((bf16[64,512]{1,0:T(8,128)(2,1)S(1)}, bf16[64,512]{1,0:T(8,128)(2,1)S(1)}, u32[]{:S(2)}, u32[]{:S(2)}) %collective-permute-start.2) | collective-permute-done | bytes 65568 | tf_op jit(solution)/shard_map/ppermute | solution.py:15
  67.9 3.8 %all_to_all.36 = bf16[64,2,256]{2,0,1:T(8,128)(2,1)S(1)} all-to-all(bf16[64,2,256]{2,0,1:T(8,128)(2,1)S(1)} %bitcast.192), channel_id=1, replica_groups=mesh['groups'=2,'space'=4,'tm'=2,'chan'=2] {'chan'}, dimensions={1} | all-to-all | bytes 131072 | tf_op jit(solution)/shard_map/all_to_all | solution.py:81
  72.1 17.4 %all-reduce.1 = (f32[16]{0:T(128)S(1)}, f32[16]{0:T(128)S(1)}) all-reduce(f32[16]{0:T(128)S(1)} %reduce_sum.85, f32[16]{0:T(128)S(1)} %reduce_sum.82), channel_id=1, replica_groups=mesh['groups'=2,'space'=4,'tm'=2,'chan'=2] {'space','tm'}, use_global_device_ids=true, to_apply=%region_13.14 | all-reduce | flops 32 | bytes 256 | tf_op jit(solution)/shard_map/psum | solution.py:49
  90.0 1.9 %all_gather.10 = bf16[2,1,64,512]{3,2,1,0:T(8,128)(2,1)S(1)} all-gather(bf16[2,1,64,256]{3,2,1,0:T(8,128)(2,1)S(1)} %multiply_convert_fusion), channel_id=1, replica_groups=mesh['groups'=2,'space'=4,'tm'=2,'chan'=2] {'chan'}, dimensions={3}, use_global_device_ids=true | all-gather | bytes 196608 | tf_op jit(solution)/shard_map/all_gather | solution.py:86
  91.9 4.1 %collective-permute-start.3 = (bf16[2,1,64,512]{3,2,1,0:T(8,128)(2,1)S(1)}, bf16[2,1,64,512]{3,2,1,0:T(8,128)(2,1)S(1)}, u32[]{:S(2)}, u32[]{:S(2)}) collective-permute-start(bf16[2,1,64,512]{3,2,1,0:T(8,128)(2,1)S(1)} %all_gather.10), channel_id=1, source_target_pairs={{0,2},{1,3},{4,6},{5,7},{8,10},{9,11},{12,14},{13,15},{16,18},{17,... | collective-permute-start | bytes 393224 | tf_op jit(solution)/shard_map/ppermute | solution.py:24
  96.0 6.4 %collective-permute-done.3 = bf16[2,1,64,512]{3,2,1,0:T(8,128)(2,1)S(1)} collective-permute-done((bf16[2,1,64,512]{3,2,1,0:T(8,128)(2,1)S(1)}, bf16[2,1,64,512]{3,2,1,0:T(8,128)(2,1)S(1)}, u32[]{:S(2)}, u32[]{:S(2)}) %collective-permute-start.3) | collective-permute-done | bytes 131104 | tf_op jit(solution)/shard_map/ppermute | solution.py:24
  102.5 1.3 collective-permute-start.4
  103.8 1.3 collective-permute-start.5
  105.1 4.1 %collective-permute-done.4 = bf16[4,1,64,512]{3,2,1,0:T(8,128)(2,1)S(1)} collective-permute-done((bf16[4,1,64,512]{3,2,1,0:T(8,128)(2,1)S(1)}, bf16[4,1,64,512]{3,2,1,0:T(8,128)(2,1)S(1)}, u32[]{:S(2)}, u32[]{:S(2)}) %collective-permute-start.4) | collective-permute-done | bytes 262176 | tf_op jit(solution)/shard_map/ppermute | solution.py:35
  109.2 4.1 %collective-permute-done.5 = bf16[4,1,64,512]{3,2,1,0:T(8,128)(2,1)S(1)} collective-permute-done((bf16[4,1,64,512]{3,2,1,0:T(8,128)(2,1)S(1)}, bf16[4,1,64,512]{3,2,1,0:T(8,128)(2,1)S(1)}, u32[]{:S(2)}, u32[]{:S(2)}) %collective-permute-start.5) | collective-permute-done | bytes 262176 | tf_op jit(solution)/shard_map/ppermute | solution.py:37
  115.5 1.3 fusion.20
  116.8 1.7 %fusion.19 = f32[128,256]{1,0:T(8,128)S(1)} fusion(bf16[128,512]{1,0:T(8,128)(2,1)S(1)} %bitcast.183, bf16[3,3,3,512,256]{4,3,2,1,0:T(8,128)(2,1)} %all-gather.2.cloned.1.call-done), kind=kOutput, calls=%fused_computation.69 | convolution fusion | flops 33554432 | bytes 524288 | tf_op jit(solution)/shard_map/dot_general | solution.py:112
  122.0 1.2 fusion.15
  123.1 1.1 fusion.14
  124.3 1.1 convolution_add_fusion.19
  125.4 1.1 convolution_add_fusion.18
  128.9 1.1 convolution_add_fusion.15
  (88 shorter events, 18.5 us)
Async XLA Ops:
  7.2 30.4 %copy-start = (bf16[512,512]{1,0:T(8,128)(2,1)S(1)}, bf16[512,512]{1,0:T(8,128)(2,1)}, u32[]{:S(2)}) copy-start(bf16[512,512]{1,0:T(8,128)(2,1)} %param.13) | copy-start | bytes 1572868
  7.2 64.5 %copy-start.2 = (bf16[2,1,64,256]{3,2,1,0:T(8,128)(2,1)S(1)}, bf16[2,1,64,256]{3,2,1,0:T(8,128)(2,1)}, u32[]{:S(2)}) copy-start(bf16[2,1,64,256]{3,2,1,0:T(8,128)(2,1)} %param.8) | copy-start | bytes 196612
  7.2 60.3 %copy-start.8 = (bf16[512,512]{1,0:T(8,128)(2,1)S(1)}, bf16[512,512]{1,0:T(8,128)(2,1)}, u32[]{:S(2)}) copy-start(bf16[512,512]{1,0:T(8,128)(2,1)} %param.14) | copy-start | bytes 1572868
  7.2 82.7 %copy-start.7 = (f32[256]{0:T(256)S(1)}, f32[256]{0:T(256)}, u32[]{:S(2)}) copy-start(f32[256]{0:T(256)} %param.10) | copy-start | bytes 3076
  7.2 108.3 %all-gather.2.cloned.1.call-start = ((), (), s32[]{:S(2)}) async-start(), calls=%async_computation.2 | async-start | bytes 10616832 | tf_op jit(solution)/shard_map/all_gather | solution.py:102
  37.8 17.1 %collective-permute-start = (bf16[64,512]{1,0:T(8,128)(2,1)S(1)}, bf16[64,512]{1,0:T(8,128)(2,1)S(1)}, u32[]{:S(2)}, u32[]{:S(2)}) collective-permute-start(bf16[64,512]{1,0:T(8,128)(2,1)S(1)} %convolution_convert_fusion.1), channel_id=1, source_target_pairs={{0,4},{4,8},{8,12},{12,0},{1,5},{5,9},{9,13},{13,1},{2,6},{6,10},{... | collective-permute-start | bytes 196616 | tf_op jit(solution)/shard_map/ppermute | solution.py:15
  54.8 6.5 %collective-permute-start.1 = (bf16[64,512]{1,0:T(8,128)(2,1)S(1)}, bf16[64,512]{1,0:T(8,128)(2,1)S(1)}, u32[]{:S(2)}, u32[]{:S(2)}) collective-permute-start(bf16[64,512]{1,0:T(8,128)(2,1)S(1)} %collective-permute-done), channel_id=1, source_target_pairs={{0,4},{4,8},{8,12},{12,0},{1,5},{5,9},{9,13},{13,1},{2,6},{6,10},{... | collective-permute-start | bytes 196616 | tf_op jit(solution)/shard_map/ppermute | solution.py:15
  61.3 6.1 %collective-permute-start.2 = (bf16[64,512]{1,0:T(8,128)(2,1)S(1)}, bf16[64,512]{1,0:T(8,128)(2,1)S(1)}, u32[]{:S(2)}, u32[]{:S(2)}) collective-permute-start(bf16[64,512]{1,0:T(8,128)(2,1)S(1)} %collective-permute-done.1), channel_id=1, source_target_pairs={{0,4},{4,8},{8,12},{12,0},{1,5},{5,9},{9,13},{13,1},{2,6},{6,10},{... | collective-permute-start | bytes 196616 | tf_op jit(solution)/shard_map/ppermute | solution.py:15
  91.9 10.6 %collective-permute-start.3 = (bf16[2,1,64,512]{3,2,1,0:T(8,128)(2,1)S(1)}, bf16[2,1,64,512]{3,2,1,0:T(8,128)(2,1)S(1)}, u32[]{:S(2)}, u32[]{:S(2)}) collective-permute-start(bf16[2,1,64,512]{3,2,1,0:T(8,128)(2,1)S(1)} %all_gather.10), channel_id=1, source_target_pairs={{0,2},{1,3},{4,6},{5,7},{8,10},{9,11},{12,14},{13,15},{16,18},{17,... | collective-permute-start | bytes 393224 | tf_op jit(solution)/shard_map/ppermute | solution.py:24
  102.5 6.7 %collective-permute-start.4 = (bf16[4,1,64,512]{3,2,1,0:T(8,128)(2,1)S(1)}, bf16[4,1,64,512]{3,2,1,0:T(8,128)(2,1)S(1)}, u32[]{:S(2)}, u32[]{:S(2)}) collective-permute-start(bf16[4,1,64,512]{3,2,1,0:T(8,128)(2,1)S(1)} %constant_dynamic-update-slice_fusion.8), channel_id=1, source_target_pairs={{0,4},{4,8},{8,12},{1,5},{5,9},{9,13},{2,6},{6,10},{10,14},{3,7},{... | collective-permute-start | bytes 786440 | tf_op jit(solution)/shard_map/ppermute | solution.py:35
  103.8 9.5 %collective-permute-start.5 = (bf16[4,1,64,512]{3,2,1,0:T(8,128)(2,1)S(1)}, bf16[4,1,64,512]{3,2,1,0:T(8,128)(2,1)S(1)}, u32[]{:S(2)}, u32[]{:S(2)}) collective-permute-start(bf16[4,1,64,512]{3,2,1,0:T(8,128)(2,1)S(1)} %constant_dynamic-update-slice_fusion.8), channel_id=1, source_target_pairs={{4,0},{8,4},{12,8},{5,1},{9,5},{13,9},{6,2},{10,6},{14,10},{7,3},{... | collective-permute-start | bytes 786440 | tf_op jit(solution)/shard_map/ppermute | solution.py:37
  115.5 14.5 %copy-start.1 = (bf16[3,3,3,512,256]{4,3,2,1,0:T(8,128)(2,1)S(1)}, bf16[3,3,3,512,256]{4,3,2,1,0:T(8,128)(2,1)}, u32[]{:S(2)}) copy-start(bf16[3,3,3,512,256]{4,3,2,1,0:T(8,128)(2,1)} %all-gather.2.cloned.1.call-done) | copy-start | bytes 21233668
  115.5 15.8 %copy-start.6 = (bf16[2,1,64,512]{3,2,1,0:T(8,128)(2,1)S(1)}, bf16[2,1,64,512]{3,2,1,0:T(8,128)(2,1)}, u32[]{:S(2)}) copy-start(bf16[2,1,64,512]{3,2,1,0:T(8,128)(2,1)} %get-tuple-element.38) | copy-start | bytes 393220
  115.5 16.8 %copy-start.5 = (bf16[2,1,64,512]{3,2,1,0:T(8,128)(2,1)S(1)}, bf16[2,1,64,512]{3,2,1,0:T(8,128)(2,1)}, u32[]{:S(2)}) copy-start(bf16[2,1,64,512]{3,2,1,0:T(8,128)(2,1)} %get-tuple-element.35) | copy-start | bytes 393220
  115.5 17.2 %copy-start.4 = (bf16[2,1,64,512]{3,2,1,0:T(8,128)(2,1)S(1)}, bf16[2,1,64,512]{3,2,1,0:T(8,128)(2,1)}, u32[]{:S(2)}) copy-start(bf16[2,1,64,512]{3,2,1,0:T(8,128)(2,1)} %get-tuple-element.37) | copy-start | bytes 393220
  121.9 11.8 %copy-start.3 = (bf16[2,1,64,512]{3,2,1,0:T(8,128)(2,1)S(1)}, bf16[2,1,64,512]{3,2,1,0:T(8,128)(2,1)}, u32[]{:S(2)}) copy-start(bf16[2,1,64,512]{3,2,1,0:T(8,128)(2,1)} %get-tuple-element.34) | copy-start | bytes 393220
Sparse Core Ops, SparseCore 0:
  9.6 93.2 all-gather.1
